TPU v7x, 256 devices: a whole 4x4x8 slice. The times are simulated.
256 devices in a mesh: seq: 32 (over x, z), head: 8 (over y, core).
Axes of the slice: x: 4, y: 4, z: 8, core: 2. Of those that a mesh axis runs over, the one named last changes fastest.
Arguments:
- queries: bfloat16 [65536, 4096], P(('seq', 'head')), may hold values from -6 to 6
- keys: bfloat16 [65536, 4096], P(('seq', 'head')), may hold values from -6 to 6
- values: bfloat16 [65536, 4096], P(('seq', 'head')), may hold values from -6 to 6
- spikes: int32 [65536, 4096], P(('seq', 'head')), may hold values from 0 to 26
- gain: float32 [4096], P('head'), may hold values from 0.1 to 1.9
Outputs:
- attended: bfloat16 [65536, 4096], P('seq', 'head')
- cache: float32 [32, 32, 128, 128], P('seq', 'head')
Inputs may be any that keep to these rules, and one draw needn't show every extreme that they name: spikes codes count_query + 3 count_key + 9 count_value with each count 0, 1 or 2.
All inputs are finite; a program needn't handle non-finite values.
Results may differ from a plain program's by a relative error of at most 0.0027.
Values may be sent and summed in bfloat16 or wider, within the bound.
A program may use at most 128 MiB of HBM per device.

v0:
```python
import jax
import jax.numpy as jnp
from jax import lax
from jax.sharding import PartitionSpec as P

HD = 128


def entering(value, axis, join, neutral):
    count, mine = (lax.axis_size(axis), lax.axis_index(axis))
    pieces = lax.all_gather(value, axis)
    running = jnp.full_like(value, 0) + jnp.asarray(neutral, value.dtype)

    def hop(position, running):
        longer = join(running, pieces[position])
        return jnp.where(position < mine, longer, running)

    return lax.fori_loop(0, count - 1, hop, running)


def decode_counts(spikes):
    return (spikes % 3, spikes // 3 % 3, spikes // 9)


def add_states(earlier, later):
    return earlier + later


def per_device(queries, keys, values, spikes, gain):
    count_query, count_key, count_value = decode_counts(spikes)
    spiked_query = queries * count_query.astype(jnp.bfloat16)
    spiked_key = keys * count_key.astype(jnp.bfloat16)
    spiked_value = values * count_value.astype(jnp.bfloat16)
    query_block, key_block, value_block = (
        lax.all_to_all(spiked_query, "head", split_axis=1, concat_axis=0, tiled=True),
        lax.all_to_all(spiked_key, "head", split_axis=1, concat_axis=0, tiled=True),
        lax.all_to_all(spiked_value, "head", split_axis=1, concat_axis=0, tiled=True),
    )
    block_rows = key_block.shape[0]
    head_count = key_block.shape[1] // HD
    key_heads = key_block.reshape(block_rows, head_count, HD)
    value_heads = value_block.reshape(block_rows, head_count, HD)
    states = jnp.einsum("shd,she->hde", key_heads, value_heads, preferred_element_type=jnp.float32)
    zeros_state = jnp.zeros_like(states)
    block_index = lax.axis_index("seq")
    earlier_state = entering(states, "seq", add_states, zeros_state)
    inclusive = earlier_state + states
    seen_tokens = ((block_index + 1) * block_rows).astype(jnp.float32)
    cache = (inclusive * lax.rsqrt(seen_tokens))[None]
    query_heads = query_block.reshape(block_rows, head_count, HD)
    score_scale = HD ** (-0.5)
    tile_rows = min(1024, block_rows)
    tile_count = block_rows // tile_rows
    causal = lax.broadcasted_iota(jnp.int32, (tile_rows, tile_rows), 0) >= lax.broadcasted_iota(
        jnp.int32, (tile_rows, tile_rows), 1
    )
    results = []
    for row_tile in range(tile_count):
        query_tile = query_heads[row_tile * tile_rows : (row_tile + 1) * tile_rows]
        total = (
            jnp.einsum(
                "thd,hde->the",
                query_tile.astype(jnp.float32),
                earlier_state,
                precision=lax.Precision.HIGHEST,
            )
            * score_scale
        )
        for col_tile in range(row_tile + 1):
            key_tile = key_heads[col_tile * tile_rows : (col_tile + 1) * tile_rows]
            value_tile = value_heads[col_tile * tile_rows : (col_tile + 1) * tile_rows]
            scores = (
                jnp.einsum("thd,shd->hts", query_tile, key_tile, preferred_element_type=jnp.float32)
                * score_scale
            )
            if col_tile == row_tile:
                scores = jnp.where(causal[None], scores, 0.0)
            weights = scores.astype(jnp.bfloat16)
            total = total + jnp.einsum(
                "hts,shd->thd", weights, value_tile, preferred_element_type=jnp.float32
            )
        results.append(total)
    raw = jnp.concatenate(results, axis=0)
    head_gain = gain.reshape(head_count, HD)
    normed = raw * lax.rsqrt(jnp.mean(raw * raw, axis=-1, keepdims=True) + 1e-06) * head_gain
    return (normed.reshape(block_rows, head_count * HD).astype(jnp.bfloat16), cache)


def solution(mesh):
    in_specs = (
        P(("seq", "head"), None),
        P(("seq", "head"), None),
        P(("seq", "head"), None),
        P(("seq", "head"), None),
        P("head"),
    )
    out_specs = (P("seq", "head"), P("seq", "head", None, None))
    return jax.shard_map(
        per_device, mesh=mesh, in_specs=in_specs, out_specs=out_specs, check_vma=False
    )
```

profile of v0, /device:TPU:1, one launch (start us, length us, event | category | flops | bytes accessed | tf_op | source)
XLA Modules:
  0.0 254.5 jit_solution(6090944371478610126)
XLA Ops:
  7.2 12.5 %fusion.11 = (bf16[256,4096]{1,0:T(8,128)(2,1)}, bf16[256,4096]{1,0:T(8,128)(2,1)S(1)}, bf16[256,4096]{1,0:T(8,128)(2,1)}) fusion(bf16[256,4096]{1,0:T(8,128)(2,1)} %param.7, s32[256,4096]{1,0:T(8,128)} %param.10, bf16[256,4096]{1,0:T(8,128)(2,1)} %param.9, bf16[256,4096]{1,0:T(8,128)(2,1)} %param.8), kind=kLoop, calls=%fused_computation.25 | loop fusion | flops 40894464 | bytes 16777216 | tf_op jit(solution)/shard_map/mul | solution.py:31
  22.1 6.7 %all-to-all-start.1 = ((bf16[256,8,512]{0,2,1:T(8,128)(2,1)}), bf16[256,8,512]{0,2,1:T(8,128)(2,1)S(1)}, u32[]{:S(2)}, u32[]{:S(2)}) async-start(bf16[256,8,512]{0,2,1:T(8,128)(2,1)} %bitcast.55), calls=%async_computation.1 | async-start | bytes 4194304 | tf_op jit(solution)/shard_map/all_to_all | solution.py:37
  28.8 4.1 %copy.41 = bf16[256,4096]{0,1:T(8,128)(2,1)} copy(bf16[256,4096]{1,0:T(8,128)(2,1)} %get-tuple-element.107) | data formatting | bytes 4194304 | tf_op jit(solution)/shard_map/mul | solution.py:32
  32.9 22.2 %all-to-all-done.1 = bf16[256,8,512]{0,2,1:T(8,128)(2,1)S(1)} async-done(((bf16[256,8,512]{0,2,1:T(8,128)(2,1)}), bf16[256,8,512]{0,2,1:T(8,128)(2,1)S(1)}, u32[]{:S(2)}, u32[]{:S(2)}) %all-to-all-start.1) | async-done | bytes 2097184 | tf_op jit(solution)/shard_map/all_to_all | solution.py:37
  56.4 4.5 %all-to-all-start = ((bf16[256,8,512]{0,2,1:T(8,128)(2,1)}), bf16[256,8,512]{0,2,1:T(8,128)(2,1)S(1)}, u32[]{:S(2)}, u32[]{:S(2)}) async-start(bf16[256,8,512]{0,2,1:T(8,128)(2,1)} %bitcast.54), calls=%async_computation | async-start | bytes 4194304 | tf_op jit(solution)/shard_map/all_to_all | solution.py:36
  60.9 4.1 %copy.44 = bf16[8,256,512]{1,0,2:T(8,128)(2,1)} copy(bf16[8,256,512]{1,2,0:T(8,128)(2,1)} %bitcast.46) | data formatting | bytes 4194304 | tf_op jit(solution)/shard_map/all_to_all | solution.py:37
  65.0 4.2 %reshape.52 = bf16[2048,4,128]{0,2,1:T(8,128)(2,1)} reshape(bf16[8,256,512]{1,0,2:T(8,128)(2,1)} %copy.44) | data formatting | bytes 4194304 | tf_op jit(solution)/shard_map/reshape | solution.py:42
  69.1 17.9 %all-to-all-done = bf16[256,8,512]{0,2,1:T(8,128)(2,1)S(1)} async-done(((bf16[256,8,512]{0,2,1:T(8,128)(2,1)}), bf16[256,8,512]{0,2,1:T(8,128)(2,1)S(1)}, u32[]{:S(2)}, u32[]{:S(2)}) %all-to-all-start) | async-done | bytes 2097184 | tf_op jit(solution)/shard_map/all_to_all | solution.py:36
  87.1 2.5 copy.42
  89.6 4.2 %reshape.51 = bf16[2048,4,128]{0,2,1:T(8,128)(2,1)} reshape(bf16[8,256,512]{1,0,2:T(8,128)(2,1)} %copy.42) | data formatting | bytes 4194304 | tf_op jit(solution)/shard_map/reshape | solution.py:41
  93.8 3.6 %fusion.36 = f32[4,128,128]{2,1,0:T(8,128)} fusion(bf16[2048,4,128]{0,2,1:T(8,128)(2,1)} %reshape.51, bf16[2048,4,128]{0,2,1:T(8,128)(2,1)} %reshape.52), kind=kOutput, calls=%fused_computation.49 | convolution fusion | flops 268435456 | bytes 4456448 | tf_op jit(solution)/shard_map/shd,she->hde/dot_general | solution.py:43
  97.5 3.1 %copy.93 = bf16[32,8,8,512]{3,2,0,1:T(8,128)(2,1)} copy(bf16[32,8,8,512]{3,2,1,0:T(8,128)(2,1)} %bitcast.56) | data formatting | bytes 4194304 | tf_op jit(solution)/shard_map/all_to_all | solution.py:35
  100.6 5.2 %all-to-all-start.2 = ((bf16[256,8,512]{2,0,1:T(8,128)(2,1)}), bf16[256,8,512]{2,0,1:T(8,128)(2,1)}, u32[]{:S(2)}, u32[]{:S(2)}) async-start(bf16[256,8,512]{2,0,1:T(8,128)(2,1)} %bitcast.53), calls=%async_computation.2 | async-start | bytes 4194304 | tf_op jit(solution)/shard_map/all_to_all | solution.py:35
  107.1 25.0 %all-to-all-done.2 = bf16[256,8,512]{2,0,1:T(8,128)(2,1)} async-done(((bf16[256,8,512]{2,0,1:T(8,128)(2,1)}), bf16[256,8,512]{2,0,1:T(8,128)(2,1)}, u32[]{:S(2)}, u32[]{:S(2)}) %all-to-all-start.2) | async-done | bytes 2097184 | tf_op jit(solution)/shard_map/all_to_all | solution.py:35
  132.1 2.7 %fusion.33 = (bf16[4,256,512]{2,1,0:T(8,128)(2,1)}, bf16[4,256,512]{2,1,0:T(8,128)(2,1)S(1)}) fusion(bf16[8,256,512]{2,1,0:T(8,128)(2,1)} %bitcast.5), kind=kLoop, calls=%fused_computation.46 | loop fusion | bytes 4194304 | tf_op jit(solution)/shard_map/slice | solution.py:59
  138.3 2.6 %fusion.35 = (bf16[4,256,512]{1,2,0:T(8,128)(2,1)S(1)}, bf16[4,256,512]{1,2,0:T(8,128)(2,1)}) fusion(bf16[8,256,512]{1,2,0:T(8,128)(2,1)} %bitcast.47), kind=kLoop, calls=%fused_computation.48 | loop fusion | bytes 4194304 | tf_op jit(solution)/shard_map/slice | solution.py:71
  152.6 8.0 %fusion.8 = f32[4,128,1024]{2,1,0:T(8,128)} fusion(bf16[1024,4,128]{0,2,1:T(8,128)(2,1)} %slice.41, bf16[1024,4,128]{2,1,0:T(4,128)(2,1)} %slice.43, bf16[1024,4,128]{2,1,0:T(4,128)(2,1)S(1)} %copy-done.5), kind=kOutput, calls=%fused_computation.22 | convolution fusion | flops 2155872256 | bytes 5242880 | tf_op jit(solution)/shard_map/hts,shd->thd/dot_general | solution.py:79
  160.6 8.1 %fusion.9 = f32[4,128,1024]{2,1,0:T(8,128)} fusion(bf16[1024,4,128]{0,2,1:T(8,128)(2,1)} %slice.41, pred[1024,1024]{1,0:T(8,128)(4,1)S(1)} %copy-done.10, bf16[1024,4,128]{2,1,0:T(4,128)(2,1)} %slice.43, bf16[1024,4,128]{2,1,0:T(4,128)(2,1)S(1)} %copy-done.4), kind=kOutput, calls=%fused_computation.23 | convolution fusion | flops 2160066560 | bytes 6291456 | tf_op jit(solution)/shard_map/hts,shd->thd/dot_general | solution.py:79
  168.7 8.0 %fusion.10 = f32[4,128,1024]{2,1,0:T(8,128)} fusion(bf16[1024,4,128]{0,2,1:T(8,128)(2,1)} %slice.47, pred[1024,1024]{1,0:T(8,128)(4,1)S(1)} %copy-done.10, bf16[1024,4,128]{2,1,0:T(4,128)(2,1)} %slice.49, bf16[1024,4,128]{2,1,0:T(4,128)(2,1)S(1)} %copy-done.5), kind=kOutput, calls=%fused_computation.24 | convolution fusion | flops 2160066560 | bytes 6291456 | tf_op jit(solution)/shard_map/hts,shd->thd/dot_general | solution.py:79
  176.7 18.5 %all-gather.3.cloned.1.call-done = f32[128,128,128]{2,1,0:T(8,128)} async-done(((f32[4,128,128]{2,1,0:T(8,128)}), f32[128,128,128]{2,1,0:T(8,128)}) %all-gather.3.cloned.1.call-update) | async-done | bytes 8388624 | tf_op jit(solution)/shard_map/all_gather | solution.py:11
  195.1 33.2 %while.14 = (s32[]{:T(128)}, f32[4,128,128]{2,1,0:T(8,128)S(1)}, s32[]{:T(128)}, f32[32,4,128,128]{3,2,1,0:T(8,128)}, s32[]{:T(128)}, /*index=5*/s32[]{:T(128)}) while((s32[]{:T(128)}, f32[4,128,128]{2,1,0:T(8,128)S(1)}, s32[]{:T(128)}, f32[32,4,128,128]{3,2,1,0:T(8,128)}, s32[]{:T(128)}, /*index=5*/s32[]{:T(128)}) %tuple.46), condition=%wide.region_1.2_spmd.clone, body=%wide.region_0.1_spmd.clone.sunk | while | flops 196612 | bytes 786533 | solution.py:18
  229.1 3.1 %multiply_add_fusion = f32[4,128,1024]{2,1,0:T(8,128)S(1)} fusion(f32[4,128,1024]{2,1,0:T(8,128)} %fusion.9, f32[4,128,128]{2,1,0:T(8,128)S(1)} %get-tuple-element.81, bf16[1024,4,128]{2,1,0:T(4,128)(2,1)S(1)} %copy-done.4), kind=kOutput, calls=%fused_computation.28 | convolution fusion | flops 806354944 | bytes 5505024 | tf_op jit(solution)/shard_map/thd,hde->the/dot_general | solution.py:61
  235.8 2.9 %copy.62 = f32[1024,512]{1,0:T(8,128)} copy(f32[1024,512]{0,1:T(8,128)} %bitcast.51) | data formatting | bytes 4194304 | tf_op jit(solution)/shard_map/concatenate | solution.py:83
  240.5 4.6 %mul.67 = f32[2048,4,128]{2,1,0:T(4,128)S(1)} broadcast(f32[2048,4]{1,0:T(8,128)S(1)} %copy.63), dimensions={0,1} | broadcast | bytes 4227072 | tf_op jit(solution)/shard_map/mul | solution.py:85
  (78 shorter events, 60.9 us)
Async XLA Ops:
  22.1 32.9 %all-to-all-start.1 = ((bf16[256,8,512]{0,2,1:T(8,128)(2,1)}), bf16[256,8,512]{0,2,1:T(8,128)(2,1)S(1)}, u32[]{:S(2)}, u32[]{:S(2)}) async-start(bf16[256,8,512]{0,2,1:T(8,128)(2,1)} %bitcast.55), calls=%async_computation.1 | async-start | bytes 4194304 | tf_op jit(solution)/shard_map/all_to_all | solution.py:37
  55.1 1.3 copy-start
  56.4 30.7 %all-to-all-start = ((bf16[256,8,512]{0,2,1:T(8,128)(2,1)}), bf16[256,8,512]{0,2,1:T(8,128)(2,1)S(1)}, u32[]{:S(2)}, u32[]{:S(2)}) async-start(bf16[256,8,512]{0,2,1:T(8,128)(2,1)} %bitcast.54), calls=%async_computation | async-start | bytes 4194304 | tf_op jit(solution)/shard_map/all_to_all | solution.py:36
  60.9 134.3 %all-gather.3.cloned.1.call-start = ((), (), s32[]{:S(2)}) async-start(), calls=%async_computation.3 | async-start | bytes 8650752 | tf_op jit(solution)/shard_map/all_gather | solution.py:11
  100.6 31.5 %all-to-all-start.2 = ((bf16[256,8,512]{2,0,1:T(8,128)(2,1)}), bf16[256,8,512]{2,0,1:T(8,128)(2,1)}, u32[]{:S(2)}, u32[]{:S(2)}) async-start(bf16[256,8,512]{2,0,1:T(8,128)(2,1)} %bitcast.53), calls=%async_computation.2 | async-start | bytes 4194304 | tf_op jit(solution)/shard_map/all_to_all | solution.py:35
  148.0 4.6 %copy-start.5 = (bf16[1024,4,128]{2,1,0:T(4,128)(2,1)S(1)}, bf16[1024,4,128]{2,1,0:T(4,128)(2,1)}, u32[]{:S(2)}) copy-start(bf16[1024,4,128]{2,1,0:T(4,128)(2,1)} %slice.45) | copy-start | bytes 3145732
  152.6 8.0 %copy-start.4 = (bf16[1024,4,128]{2,1,0:T(4,128)(2,1)S(1)}, bf16[1024,4,128]{2,1,0:T(4,128)(2,1)}, u32[]{:S(2)}) copy-start(bf16[1024,4,128]{2,1,0:T(4,128)(2,1)} %slice.39) | copy-start | bytes 3145732
  152.6 8.0 %copy-start.10 = (pred[1024,1024]{1,0:T(8,128)(4,1)S(1)}, pred[1024,1024]{1,0:T(8,128)(4,1)}, u32[]{:S(2)}) copy-start(pred[1024,1024]{1,0:T(8,128)(4,1)} %iota_compare_fusion) | copy-start | bytes 3145732
  176.7 51.7 %copy-start.7 = (f32[4,128,128]{2,1,0:T(8,128)S(1)}, f32[4,128,128]{2,1,0:T(8,128)}, u32[]{:S(2)}) copy-start(f32[4,128,128]{2,1,0:T(8,128)} %fusion.36) | copy-start | bytes 786436
  228.3 3.9 %copy-start.6 = (bf16[1024,4,128]{2,1,0:T(4,128)(2,1)S(1)}, bf16[1024,4,128]{2,1,0:T(4,128)(2,1)}, u32[]{:S(2)}) copy-start(bf16[1024,4,128]{2,1,0:T(4,128)(2,1)} %slice.45) | copy-start | bytes 3145732
  228.3 3.9 %copy-start.8 = (f32[4,128,1024]{2,1,0:T(8,128)S(1)}, f32[4,128,1024]{2,1,0:T(8,128)}, u32[]{:S(2)}) copy-start(f32[4,128,1024]{2,1,0:T(8,128)} %fusion.8) | copy-start | bytes 6291460
  228.4 3.9 %copy-start.9 = (f32[4,128,1024]{2,1,0:T(8,128)S(1)}, f32[4,128,1024]{2,1,0:T(8,128)}, u32[]{:S(2)}) copy-start(f32[4,128,1024]{2,1,0:T(8,128)} %fusion.10) | copy-start | bytes 6291460
  233.6 1.3 copy-start.1
  238.7 6.5 %copy-start.11 = (f32[512]{0:T(512)S(1)}, f32[512]{0:T(512)}, u32[]{:S(2)}) copy-start(f32[512]{0:T(512)} %param.11) | copy-start | bytes 6148
  240.5 4.7 %copy-start.2 = (f32[1024,512]{1,0:T(8,128)S(1)}, f32[1024,512]{1,0:T(8,128)}, u32[]{:S(2)}) copy-start(f32[1024,512]{1,0:T(8,128)} %copy.62) | copy-start | bytes 6291460
  240.5 4.7 %copy-start.3 = (f32[1024,512]{1,0:T(8,128)S(1)}, f32[1024,512]{1,0:T(8,128)}, u32[]{:S(2)}) copy-start(f32[1024,512]{1,0:T(8,128)} %copy.61) | copy-start | bytes 6291460
Sparse Core Ops, SparseCore 0:
  97.6 97.5 all-gather.2
where the time goes:
time: 256 us; the launch traced here: 254 us
  waiting for transfers between devices  83.6 us (33%)
  local copies, waits for them, and re-layouts  57.5 us (22%)
  other arithmetic  49.7 us (19%)
  matrix products  32.1 us (13%)
  starting transfers between devices  16.4 us (6%)
  between operations  14.2 us (6%)
    select_n x31, other arithmetic, hop(): return jnp.where(position < mine, longer, running)  32.3 us
    all_to_all x1, waiting for transfers between devices, per_device(): lax.all_to_all(spiked_query, 'head', split_axis=1, concat_axis=0, tiled=T...  25 us
    dot_general x3, matrix products, per_device(): jnp.einsum('hts,shd->thd', weights, value_tile, preferred_element_type=jn...  24.1 us
    all_to_all x1, waiting for transfers between devices, per_device(): lax.all_to_all(spiked_value, 'head', split_axis=1, concat_axis=0, tiled=T...  22.2 us
    all_gather x1, waiting for transfers between devices, entering(): pieces = lax.all_gather(value, axis)  18.5 us
    all_to_all x1, waiting for transfers between devices, per_device(): lax.all_to_all(spiked_key, 'head', split_axis=1, concat_axis=0, tiled=True)  17.9 us
    mul x1, other arithmetic, per_device(): spiked_query = queries * count_query.astype(jnp.bfloat16)  12.5 us
    slice x5, local copies, waits for them, and re-layouts, per_device(): value_tile = value_heads[col_tile * tile_rows:(col_tile + 1) * tile_rows]  8.6 us
  transfers between devices with their start and end apart: 4, of which 4 were waited for; matrix products, arithmetic and copies ran while one was open for 24% of the time, Pallas kernels for 0%

commit v1 on v0

v1 whole, which is shorter than its diff:
```python
import functools

import jax
import jax.numpy as jnp
from jax import lax
from jax.experimental import pallas as pl
from jax.experimental.pallas import tpu as pltpu
from jax.sharding import PartitionSpec as P

HD = 128
NX, NZ, NY, NC = 4, 8, 4, 2
NH = NY * NC
NK = 4
ROWS = 256
BLOCK = 2048
ZR = HD // NZ
SCALE = HD ** (-0.5)
f32, bf16 = jnp.float32, jnp.bfloat16


def dot(a, b, dims):
    return lax.dot_general(a, b, (dims, ((), ())), preferred_element_type=f32)


def kernel(q_ref, k_ref, v_ref, sp_ref, g_ref, out_ref, cache_ref,
           qb, kb, vb, sb, lb, S, RC, CS, T1, TZ, Z1, ZT, XB, E2, EB, PB, T3, PF, SP, OB, GB,
           in_sem, own_sem, g_s, g_r, c1_s, c1_r, t1_s, t1_r, z1_s, z1_r, x_s, x_r, z2_s, z2_r,
           t3_s, t3_r, c2_s, c2_r, o_s, o_r):
    s = lax.axis_index("seq")
    h = lax.axis_index("head")
    x, z = s // NZ, s % NZ
    y, c = h // NC, h % NC

    def at_y(d):
        return s, ((y + d) % NY) * NC + c

    def at_h(d):
        return s, (h + d) % NH

    def at_z(d):
        return x * NZ + (z + d) % NZ, h

    def at_x(d):
        return ((x + d) % NX) * NZ + z, h

    partner = (s, y * NC + 1 - c)

    def dev(p):
        return {"seq": p[0], "head": p[1]}

    sent = []

    def send(src, dst, ss, rs, to):
        cp = pltpu.make_async_remote_copy(src_ref=src, dst_ref=dst, send_sem=ss, recv_sem=rs,
                                          device_id=dev(to), device_id_type=pl.DeviceIdType.MESH)
        cp.start()
        sent.append(cp)
        return cp

    peers = [at_h(d) for d in range(1, NH)] + [at_z(d) for d in range(1, NZ)] + [at_x(d) for d in range(1, NX)]
    barrier = pltpu.get_barrier_semaphore()
    for p in peers:
        pl.semaphore_signal(barrier, inc=1, device_id=dev(p), device_id_type=pl.DeviceIdType.MESH)

    arrays = ((sp_ref, sb), (q_ref, qb), (k_ref, kb), (v_ref, vb))
    for k in range(NK):
        for a, (src, dst) in enumerate(arrays):
            for g in range(NH):
                pltpu.make_async_copy(src.at[:, pl.ds((g * NK + k) * HD, HD)], dst.at[k, g], in_sem.at[k, a]).start()

    c1, t1, z1, xc, z2, t3, c2, oc = ({} for _ in range(8))

    def stage_a(k):
        for a, (src, dst) in enumerate(arrays):
            pltpu.make_async_copy(dst.at[k], dst.at[k], in_sem.at[k, a]).wait()

        def decode(i, _):
            g = i // 4
            rows = pl.ds(pl.multiple_of((i % 4) * 64, 64), 64)
            t = sb[k, g, rows, :].astype(f32)
            cv = jnp.floor(t * 0.1112)
            r = t - 9.0 * cv
            ck = jnp.floor(r * 0.334)
            cq = r - 3.0 * ck
            qb[k, g, rows, :] = qb[k, g, rows, :] * cq.astype(bf16)
            kb[k, g, rows, :] = kb[k, g, rows, :] * ck.astype(bf16)
            vb[k, g, rows, :] = vb[k, g, rows, :] * cv.astype(bf16)
            return 0

        lax.fori_loop(0, NH * 4, decode, 0, unroll=2)

        def states(yy, _):
            for cc in range(NC):
                S[k, cc, yy] = dot(kb[k, yy * NC + cc], vb[k, yy * NC + cc], ((0,), (0,)))
            return 0

        lax.fori_loop(0, NY, states, 0)

    def send_a(k):
        c1[k] = send(S.at[k, 1 - c], RC.at[k], c1_s.at[k], c1_r.at[k], partner)

    def stage_c(k):
        c1[k].wait_recv()
        for yy in range(NY):
            CS[k, yy] = S[k, c, yy] + RC[k, yy]
        t1[k] = [send(CS.at[k, (y + d) % NY], T1.at[k, y], t1_s.at[k, d - 1], t1_r.at[k, d - 1], at_y(d)) for d in range(1, NY)]
        T1[k, y] = CS[k, y]

    def stage_l(k):
        causal = lax.broadcasted_iota(jnp.int32, (ROWS, ROWS), 0) >= lax.broadcasted_iota(jnp.int32, (ROWS, ROWS), 1)

        def local(g, _):
            scores = dot(qb[k, g], kb[k, g], ((1,), (1,))) * SCALE
            weights = jnp.where(causal, scores, 0.0).astype(bf16)
            lb[k, g] = dot(weights, vb[k, g], ((1,), (0,)))
            return 0

        lax.fori_loop(0, NH, local, 0)

    def stage_d(k):
        for cp in t1[k]:
            cp.wait_recv()
        total = T1[k, 0] + T1[k, 1] + T1[k, 2] + T1[k, 3]
        TZ[k] = total.reshape(NZ, ZR, HD)
        z1[k] = [send(TZ.at[k, (z + d) % NZ], Z1.at[k, z], z1_s.at[k, d - 1], z1_r.at[k, d - 1], at_z(d)) for d in range(1, NZ)]
        Z1[k, z] = TZ[k, z]

    def stage_x(k):
        for cp in z1[k]:
            cp.wait_recv()
        total = Z1[k, 0]
        for zz in range(1, NZ):
            total = total + Z1[k, zz]
        ZT[k] = total
        xc[k] = [send(ZT.at[k], XB.at[k, x], x_s.at[k, d - 1], x_r.at[k, d - 1], at_x(d)) for d in range(1, NX)]
        XB[k, x] = total

    def stage_y(k):
        for cp in xc[k]:
            cp.wait_recv()
        run = jnp.zeros((ZR, HD), f32)
        for xx in range(NX - 1):
            run = run + jnp.where(xx < x, XB[k, xx], 0.0)
        for zz in range(NZ):
            E2[k, zz] = run
            run = run + Z1[k, zz]
        z2[k] = [send(E2.at[k, (z + d) % NZ], EB.at[k, z], z2_s.at[k, d - 1], z2_r.at[k, d - 1], at_z(d)) for d in range(1, NZ)]
        EB[k, z] = E2[k, z]

    def stage_f(k):
        for cp in z2[k]:
            cp.wait_recv()
        run = EB[k].reshape(HD, HD)
        for yy in range(NY):
            PB[k, yy] = run
            run = run + T1[k, yy]
        t3[k] = [send(PB.at[k, (y + d) % NY], T3.at[k, y], t3_s.at[k, d - 1], t3_r.at[k, d - 1], at_y(d)) for d in range(1, NY)]
        T3[k, y] = PB[k, y]
        seen = jnp.full((8, HD), (s + 1) * BLOCK, jnp.int32).astype(f32)
        cache_ref[0, k] = (run.reshape(HD // 8, 8, HD) * lax.rsqrt(seen)).reshape(HD, HD)

    def stage_g(k):
        for cp in t3[k]:
            cp.wait_recv()
        for yy in range(NY):
            base = T3[k, yy]
            first = jnp.where(c == 0, S[k, 0, yy], RC[k, yy])
            after = base + first
            PF[k, c, yy] = jnp.where(c == 0, base, after)
            SP[k, yy] = jnp.where(c == 0, after, base)
        c2[k] = send(SP.at[k], PF.at[k, c], c2_s.at[k], c2_r.at[k], partner)

    def stage_h(k):
        c2[k].wait_recv()

        def final(yy, _):
            for cc in range(NC):
                g = yy * NC + cc
                p = PF[k, cc, yy]
                hi = p.astype(bf16)
                lo = (p - hi.astype(f32)).astype(bf16)
                q = qb[k, g]
                carried = dot(jnp.concatenate([q, q], axis=1), jnp.concatenate([hi, lo], axis=0), ((1,), (0,)))
                raw = lb[k, g] + carried * SCALE
                mean = jnp.mean(raw * raw, axis=-1, keepdims=True)
                normed = raw * lax.rsqrt(mean + 1e-06) * GB[g, pl.ds(k, 1), :]
                OB[k, g] = normed.astype(bf16)
            return 0

        lax.fori_loop(0, NY, final, 0)
        here = out_ref.at[pl.ds(h * ROWS, ROWS), pl.ds(k * HD, HD)]
        oc[k] = [send(OB.at[k, (h + d) % NH], here, o_s.at[k, d - 1], o_r.at[k, d - 1], at_h(d)) for d in range(1, NH)]
        own = pltpu.make_async_copy(OB.at[k, h], here, own_sem.at[k])
        own.start()
        return own

    stage_a(0)
    pl.semaphore_wait(barrier, len(peers))
    send_a(0)
    GB[h] = g_ref[...]
    gains = [send(g_ref, GB.at[h], g_s.at[d - 1], g_r.at[d - 1], at_h(d)) for d in range(1, NH)]
    stage_a(1)
    send_a(1)
    stage_c(0)
    stage_a(2)
    send_a(2)
    stage_c(1)
    stage_a(3)
    send_a(3)
    stage_c(2)
    stage_c(3)
    stage_l(0)
    stage_d(0)
    stage_l(1)
    stage_d(1)
    stage_x(0)
    stage_l(2)
    stage_d(2)
    stage_x(1)
    stage_y(0)
    stage_l(3)
    stage_d(3)
    stage_x(2)
    stage_y(1)
    stage_f(0)
    stage_x(3)
    stage_y(2)
    stage_f(1)
    stage_y(3)
    stage_g(0)
    stage_f(2)
    for cp in gains:
        cp.wait_recv()
    own = [stage_h(0)]
    stage_g(1)
    stage_f(3)
    own.append(stage_h(1))
    stage_g(2)
    own.append(stage_h(2))
    stage_g(3)
    own.append(stage_h(3))
    for k in range(NK):
        own[k].wait()
        for cp in oc[k]:
            cp.wait_recv()
    for cp in sent:
        cp.wait_send()


def per_device(queries, keys, values, spikes, gain):
    vmem, dma = pltpu.VMEM, pltpu.SemaphoreType.DMA
    anywhere = pl.BlockSpec(memory_space=pl.ANY)
    inside = pl.BlockSpec(memory_space=pltpu.VMEM)
    state = vmem((NK, NY, HD, HD), f32)
    slices = vmem((NK, NZ, ZR, HD), f32)
    counts = (NH - 1,), (NK,), (NK, NY - 1), (NK, NZ - 1), (NK, NX - 1), (NK, NZ - 1), (NK, NY - 1), (NK,), (NK, NH - 1)
    attended, cache = pl.pallas_call(
        kernel,
        out_shape=(jax.ShapeDtypeStruct((BLOCK, NK * HD), bf16), jax.ShapeDtypeStruct((1, NK, HD, HD), f32)),
        in_specs=[anywhere] * 4 + [inside],
        out_specs=(anywhere, inside),
        scratch_shapes=[
            vmem((NK, NH, ROWS, HD), bf16), vmem((NK, NH, ROWS, HD), bf16), vmem((NK, NH, ROWS, HD), bf16),
            vmem((NK, NH, ROWS, HD), jnp.int32), vmem((NK, NH, ROWS, HD), f32),
            vmem((NK, NC, NY, HD, HD), f32), state, state, state,
            slices, slices, vmem((NK, ZR, HD), f32), vmem((NK, NX, ZR, HD), f32), slices, slices,
            state, state, vmem((NK, NC, NY, HD, HD), f32), state,
            vmem((NK, NH, ROWS, HD), bf16), vmem((NH, NK, HD), f32),
            dma((NK, 4)), dma((NK,)),
        ] + [dma(n) for n in counts for _ in range(2)],
        compiler_params=pltpu.CompilerParams(collective_id=0, has_side_effects=True, vmem_limit_bytes=60 << 20),
    )(queries, keys, values, spikes, gain.reshape(NK, HD))
    return attended, cache


def solution(mesh):
    tokens = P(("seq", "head"), None)
    return jax.shard_map(
        per_device, mesh=mesh, in_specs=(tokens, tokens, tokens, tokens, P("head")),
        out_specs=(P("seq", "head"), P("seq", "head", None, None)), check_vma=False,
    )
```

time: 256 us -> 80.7 us (0.32)
  waiting for transfers between devices: 83.6 us -> 0 us
  Pallas kernels: 0 us -> 76.1 us
  local copies, waits for them, and re-layouts: 57.5 us -> 3.79 us
  other arithmetic: 49.7 us -> 0 us
  matrix products: 32.1 us -> 0 us
  starting transfers between devices: 16.4 us -> 0 us
  between operations: 14.2 us -> 0.65 us
    pallas_call x0 -> x1, Pallas kernels: none -> 76.1 us  [per_device(): pl.pallas_call(kernel, out_shape=(jax.ShapeDtypeStruct((BLOCK, NK * HD),...]
    all_to_all x3 -> x0, waiting for transfers between devices: 65.1 us -> none  [the longest x1 25 us: per_device(): lax.all_to_all(spiked_query, 'head', split_axis=1, concat_axis=0, tiled=T...]
    select_n x31 -> x0, other arithmetic: 32.3 us -> none  [hop(): return jnp.where(position < mine, longer, running)]
    dot_general x6 -> x0, matrix products: 32.1 us -> none  [the longest x3 24.1 us: per_device(): jnp.einsum('hts,shd->thd', weights, value_tile, preferred_element_type=jn...]
    slice x13 -> x0, local copies, waits for them, and re-layouts: 20.5 us -> none  [the longest x5 8.6 us: per_device(): value_tile = value_heads[col_tile * tile_rows:(col_tile + 1) * tile_rows]]
    all_gather x1 -> x0, waiting for transfers between devices: 18.5 us -> none  [entering(): pieces = lax.all_gather(value, axis)]
    all_to_all x3 -> x0, starting transfers between devices: 16.4 us -> none  [the longest x1 6.7 us: per_device(): lax.all_to_all(spiked_value, 'head', split_axis=1, concat_axis=0, tiled=T...]
    mul x1 -> x0, other arithmetic: 12.5 us -> none  [per_device(): spiked_query = queries * count_query.astype(jnp.bfloat16)]
  transfers between devices with their start and end apart: 4 -> 0, of which waited for: 4 -> 0; matrix products, arithmetic and copies ran while one was open for 24% -> 0% of each run, Pallas kernels for 0% -> 0%
where the time goes in v1:
time: 80.7 us; the launch traced here: 80.6 us
  Pallas kernels  76.1 us (94%)
  local copies, waits for them, and re-layouts  3.79 us (5%)
    pallas_call x1, Pallas kernels, per_device(): pl.pallas_call(kernel, out_shape=(jax.ShapeDtypeStruct((BLOCK, NK * HD),...  76.1 us
    unnamed x4, local copies, waits for them, and re-layouts  3.79 us

profile of v1, /device:TPU:1, one launch (start us, length us, event | category | flops | bytes accessed | tf_op | source)
XLA Modules:
  0.0 80.6 jit_solution(1788206903418238919)
XLA Ops:
  0.6 76.1 %shard_map.68 = (bf16[2048,512]{1,0:T(8,128)(2,1)}, f32[1,4,128,128]{3,2,1,0:T(8,128)}) custom-call(bf16[256,4096]{1,0:T(8,128)(2,1)} %q_ref.1, bf16[256,4096]{1,0:T(8,128)(2,1)} %k_ref.1, bf16[256,4096]{1,0:T(8,128)(2,1)} %v_ref.1, s32[256,4096]{1,0:T(8,128)} %sp_ref.1, f32[4,128]{1,0:T(4,128)} %bitcast.1), custom_call_target="tpu_custom_call" | custom-call | tf_op jit(solution)/shard_map/pallas_call | solution.py:257
  76.8 0.0 copy-start
  76.8 3.1 %copy.9 = bf16[2048,512]{1,0:T(8,128)(2,1)} copy(bf16[2048,512]{1,0:T(8,128)(2,1)} %get-tuple-element.4) | data formatting | bytes 4194304
  79.9 0.0 copy-done
  79.9 0.7 copy.10
Async XLA Ops:
  76.8 3.1 %copy-start = (f32[1,4,128,128]{3,2,1,0:T(8,128)S(1)}, f32[1,4,128,128]{3,2,1,0:T(8,128)}, u32[]{:S(2)}) copy-start(f32[1,4,128,128]{3,2,1,0:T(8,128)} %get-tuple-element.5) | copy-start | bytes 786436

commit v2 on v1

v2 whole, which is shorter than its diff:
```python
import functools

import jax
import jax.numpy as jnp
from jax import lax
from jax.experimental import pallas as pl
from jax.experimental.pallas import tpu as pltpu
from jax.sharding import PartitionSpec as P

HD = 128
NX, NZ, NY, NC = 4, 8, 4, 2
NH = NY * NC
NK = 4
ROWS = 256
BLOCK = 2048
ZR = HD // NZ
SCALE = HD ** (-0.5)
LAST = NK - 1
ORDER = (
    "a0", "b0", "s0", "a1", "s1", "c0", "a2", "s2", "c1", "a3", "s3", "c2", "c3", "q3",
    "l3", "d0", "d1", "l0", "d2", "d3", "x0", "x1", "l1", "y0", "x2", "y1", "l2", "x3",
    "y2", "f0", "y3", "f1", "f2", "g0", "h0", "g1", "f3", "h1", "g2", "h2", "w3",
)
f32, bf16 = jnp.float32, jnp.bfloat16


def dot(a, b, dims):
    return lax.dot_general(a, b, (dims, ((), ())), preferred_element_type=f32)


def encode(state):
    top = jnp.max(jnp.abs(state), axis=0, keepdims=True)
    scaled = state * jnp.where(top > 0.0, 1.0 / jnp.where(top > 0.0, top, 1.0), 0.0) * 32767.0
    return jnp.floor(scaled + 0.5).astype(jnp.int32).astype(jnp.int16), top


def decode_state(code, top):
    return code.astype(jnp.int32).astype(f32) * (1.0 / 32767.0) * top


def kernel(q_ref, k_ref, v_ref, sp_ref, g_ref, out_ref, cache_ref,
           qb, kb, vb, sb, lb, S, RC, CC, CM, RT, RM, T1, TZ, Z1, ZT, XB, E2, EB, PB, PC, PM, T3, TM, PF, SP, OB, GB,
           QX, LO, LX, WO,
           in_sem, own_sem, g_s, g_r, c1_s, c1_r, t1_s, t1_r, z1_s, z1_r, x_s, x_r, z2_s, z2_r,
           t3_s, t3_r, c2_s, c2_r, o_s, o_r, q_s, q_r, l_s, l_r):
    s = lax.axis_index("seq")
    h = lax.axis_index("head")
    x, z = s // NZ, s % NZ
    y, c = h // NC, h % NC

    def at_y(d):
        return s, ((y + d) % NY) * NC + c

    def at_h(d):
        return s, (h + d) % NH

    def at_z(d):
        return x * NZ + (z + d) % NZ, h

    def at_x(d):
        return ((x + d) % NX) * NZ + z, h

    partner = (s, y * NC + 1 - c)

    def dev(p):
        return {"seq": p[0], "head": p[1]}

    sent, own, gains, arrived = [], [], [], set()

    def arrive(copies):
        for cp in copies:
            cp.wait_recv()
            arrived.add(id(cp))

    def send(src, dst, ss, rs, to):
        cp = pltpu.make_async_remote_copy(src_ref=src, dst_ref=dst, send_sem=ss, recv_sem=rs,
                                          device_id=dev(to), device_id_type=pl.DeviceIdType.MESH)
        cp.start()
        sent.append(cp)
        return cp

    peers = [at_h(d) for d in range(1, NH)] + [at_z(d) for d in range(1, NZ)] + [at_x(d) for d in range(1, NX)]
    barrier = pltpu.get_barrier_semaphore()
    for p in peers:
        pl.semaphore_signal(barrier, inc=1, device_id=dev(p), device_id_type=pl.DeviceIdType.MESH)

    arrays = ((sp_ref, sb), (q_ref, qb), (k_ref, kb), (v_ref, vb))
    for k in range(NK):
        for a, (src, dst) in enumerate(arrays):
            for g in range(NH):
                pltpu.make_async_copy(src.at[:, pl.ds((g * NK + k) * HD, HD)], dst.at[k, g], in_sem.at[k, a]).start()

    c1, t1, z1, xc, z2, t3, c2, oc, ql = ({} for _ in range(9))

    def stage_a(k):
        for a, (src, dst) in enumerate(arrays):
            pltpu.make_async_copy(dst.at[k], dst.at[k], in_sem.at[k, a]).wait()

        def decode(i, _):
            g = i // 4
            rows = pl.ds(pl.multiple_of((i % 4) * 64, 64), 64)
            t = sb[k, g, rows, :].astype(f32)
            cv = jnp.floor(t * 0.1112)
            r = t - 9.0 * cv
            ck = jnp.floor(r * 0.334)
            cq = r - 3.0 * ck
            qb[k, g, rows, :] = qb[k, g, rows, :] * cq.astype(bf16)
            kb[k, g, rows, :] = kb[k, g, rows, :] * ck.astype(bf16)
            vb[k, g, rows, :] = vb[k, g, rows, :] * cv.astype(bf16)
            return 0

        lax.fori_loop(0, NH * 4, decode, 0, unroll=2)

        def states(yy, _):
            for cc in range(NC):
                S[k, cc, yy] = dot(vb[k, yy * NC + cc], kb[k, yy * NC + cc], ((0,), (0,)))
            return 0

        lax.fori_loop(0, NY, states, 0)

    def send_a(k):
        if k == LAST:
            c1[k] = send(S.at[k], RC.at[pl.ds(2 * k, 2)], c1_s.at[k], c1_r.at[k], partner)
        else:
            c1[k] = send(S.at[k, 1 - c], RC.at[2 * k + 1 - c], c1_s.at[k], c1_r.at[k], partner)

    def stage_c(k):
        arrive([c1[k]])
        for yy in range(NY):
            CC[k, yy], CM[k, yy] = encode(S[k, c, yy] + RC[2 * k + c, yy])
        t1[k] = []
        for d in range(1, NY):
            to = (y + d) % NY
            t1[k].append(send(CC.at[k, to], RT.at[k, y], t1_s.at[k, d - 1, 0], t1_r.at[k, d - 1, 0], at_y(d)))
            t1[k].append(send(CM.at[k, to], RM.at[k, y], t1_s.at[k, d - 1, 1], t1_r.at[k, d - 1, 1], at_y(d)))
        RT[k, y] = CC[k, y]
        RM[k, y] = CM[k, y]

    def apply_state(q, state):
        hi = state.astype(bf16)
        lo = (state - hi.astype(f32)).astype(bf16)
        return dot(jnp.concatenate([q, q], axis=1), jnp.concatenate([hi, lo], axis=1), ((1,), (1,))) * SCALE

    def stage_l(k):
        causal = lax.broadcasted_iota(jnp.int32, (ROWS, ROWS), 0) >= lax.broadcasted_iota(jnp.int32, (ROWS, ROWS), 1)
        second = c.astype(f32)

        def local(yy, _):
            for cc in range(NC):
                g = yy * NC + cc
                scores = dot(qb[k, g], kb[k, g], ((1,), (1,))) * SCALE
                weights = jnp.where(causal, scores, 0.0).astype(bf16)
                part = dot(weights, vb[k, g], ((1,), (0,)))
                if k == LAST:
                    part = part + apply_state(qb[k, g], RC[2 * k + cc, yy] * second)
                    LO[g] = part.astype(bf16)
                else:
                    lb[k, g] = part
            return 0

        lax.fori_loop(0, NY, local, 0)
        if k == LAST:
            for d in range(1, NH):
                ql[k].append(send(LO.at[(h + d) % NH], LX.at[h], l_s.at[d - 1], l_r.at[d - 1], at_h(d)))
            LX[h] = LO[h]

    def stage_q(k):
        ql[k] = [send(qb.at[k, (h + d) % NH], QX.at[h], q_s.at[d - 1], q_r.at[d - 1], at_h(d)) for d in range(1, NH)]
        QX[h] = qb[k, h]

    def stage_d(k):
        arrive(t1[k])
        total = None
        for yy in range(NY):
            part = decode_state(RT[k, yy], RM[k, yy])
            T1[k, yy] = part
            total = part if total is None else total + part
        TZ[k] = total.reshape(NZ, ZR, HD)
        z1[k] = [send(TZ.at[k, (z + d) % NZ], Z1.at[k, z], z1_s.at[k, d - 1], z1_r.at[k, d - 1], at_z(d)) for d in range(1, NZ)]
        Z1[k, z] = TZ[k, z]

    def stage_x(k):
        arrive(z1[k])
        total = Z1[k, 0]
        for zz in range(1, NZ):
            total = total + Z1[k, zz]
        ZT[k] = total
        xc[k] = [send(ZT.at[k], XB.at[k, x], x_s.at[k, d - 1], x_r.at[k, d - 1], at_x(d)) for d in range(1, NX)]
        XB[k, x] = total

    def stage_y(k):
        arrive(xc[k])
        run = jnp.zeros((ZR, HD), f32)
        for xx in range(NX - 1):
            run = run + jnp.where(xx < x, XB[k, xx], 0.0)
        for zz in range(NZ):
            E2[k, zz] = run
            run = run + Z1[k, zz]
        z2[k] = [send(E2.at[k, (z + d) % NZ], EB.at[k, z], z2_s.at[k, d - 1], z2_r.at[k, d - 1], at_z(d)) for d in range(1, NZ)]
        EB[k, z] = E2[k, z]

    def stage_f(k):
        arrive(z2[k])
        run = EB[k].reshape(HD, HD)
        for yy in range(NY):
            if k == LAST:
                PB[yy] = run
            else:
                PC[k, yy], PM[k, yy] = encode(run)
            run = run + T1[k, yy]
        t3[k] = []
        if k != LAST:
            for d in range(1, NY):
                to = (y + d) % NY
                t3[k].append(send(PC.at[k, to], T3.at[k, y], t3_s.at[k, d - 1, 0], t3_r.at[k, d - 1, 0], at_y(d)))
                t3[k].append(send(PM.at[k, to], TM.at[k, y], t3_s.at[k, d - 1, 1], t3_r.at[k, d - 1, 1], at_y(d)))
            T3[k, y] = PC[k, y]
            TM[k, y] = PM[k, y]
        seen = jnp.full((8, HD), (s + 1) * BLOCK, jnp.int32).astype(f32)
        cache_ref[0, k] = (run.T.reshape(HD // 8, 8, HD) * lax.rsqrt(seen)).reshape(HD, HD)

    def stage_g(k):
        arrive(t3[k])
        for yy in range(NY):
            base = decode_state(T3[k, yy], TM[k, yy])
            after = base + jnp.where(c == 0, S[k, 0, yy], RC[2 * k + 1, yy])
            PF[k, c, yy] = jnp.where(c == 0, base, after)
            SP[k, yy] = jnp.where(c == 0, after, base)
        c2[k] = send(SP.at[k], PF.at[k, c], c2_s.at[k], c2_r.at[k], partner)

    def normed(raw, gain):
        mean = jnp.mean(raw * raw, axis=-1, keepdims=True)
        return (raw * lax.rsqrt(mean + 1e-06) * gain).astype(bf16)

    def stage_h(k):
        arrive([c2[k]] + gains if k == 0 else [c2[k]])

        def final(yy, _):
            for cc in range(NC):
                g = yy * NC + cc
                OB[k, g] = normed(lb[k, g] + apply_state(qb[k, g], PF[k, cc, yy]), GB[g, pl.ds(k, 1), :])
            return 0

        lax.fori_loop(0, NY, final, 0)
        here = out_ref.at[pl.ds(h * ROWS, ROWS), pl.ds(k * HD, HD)]
        oc[k] = [send(OB.at[k, (h + d) % NH], here, o_s.at[k, d - 1], o_r.at[k, d - 1], at_h(d)) for d in range(1, NH)]
        mine = pltpu.make_async_copy(OB.at[k, h], here, own_sem.at[k])
        mine.start()
        own.append(mine)

    def stage_w(k):
        arrive(ql[k])

        def final(yy, _):
            for cc in range(NC):
                g = yy * NC + cc
                WO[g] = normed(LX[g].astype(f32) + apply_state(QX[g], PB[yy]), g_ref[pl.ds(k, 1), :])
            return 0

        lax.fori_loop(0, NY, final, 0)
        for g in range(NH):
            mine = pltpu.make_async_copy(WO.at[g], out_ref.at[pl.ds(g * ROWS, ROWS), pl.ds(k * HD, HD)], own_sem.at[NK + g])
            mine.start()
            own.append(mine)

    def stage_b(_):
        pl.semaphore_wait(barrier, len(peers))
        GB[h] = g_ref[...]
        for d in range(1, NH):
            gains.append(send(g_ref, GB.at[h], g_s.at[d - 1], g_r.at[d - 1], at_h(d)))

    stages = {"a": stage_a, "b": stage_b, "s": send_a, "c": stage_c, "l": stage_l, "d": stage_d, "x": stage_x,
              "y": stage_y, "f": stage_f, "g": stage_g, "h": stage_h, "q": stage_q, "w": stage_w}
    for step in ORDER:
        stages[step[0]](int(step[1]))
    for cp in own:
        cp.wait()
    arrive([cp for cp in sent if id(cp) not in arrived])
    for cp in sent:
        cp.wait_send()


def per_device(queries, keys, values, spikes, gain):
    vmem, dma = pltpu.VMEM, pltpu.SemaphoreType.DMA
    anywhere = pl.BlockSpec(memory_space=pl.ANY)
    inside = pl.BlockSpec(memory_space=pltpu.VMEM)
    state = vmem((NK, NY, HD, HD), f32)
    pair = vmem((NK, NC, NY, HD, HD), f32)
    code = vmem((NK, NY, HD, HD), jnp.int16)
    top = vmem((NK, NY, 1, HD), f32)
    slices = vmem((NK, NZ, ZR, HD), f32)
    rows16, head16 = vmem((NK, NH, ROWS, HD), bf16), vmem((NH, ROWS, HD), bf16)
    over_y, over_z, over_h = (NK, NY - 1, 2), (NK, NZ - 1), (NH - 1,)
    counts = over_h, (NK,), over_y, over_z, (NK, NX - 1), over_z, over_y, (NK,), (NK, NH - 1), over_h, over_h
    attended, cache = pl.pallas_call(
        kernel,
        out_shape=(vmem((BLOCK, NK * HD), bf16), vmem((1, NK, HD, HD), f32)),
        in_specs=[anywhere] * 4 + [inside],
        out_specs=(inside, inside),
        scratch_shapes=[
            rows16, rows16, rows16, vmem((NK, NH, ROWS, HD), jnp.int32), vmem((NK, NH, ROWS, HD), f32),
            pair, vmem((NK * NC, NY, HD, HD), f32), code, top, code, top, state,
            slices, slices, vmem((NK, ZR, HD), f32), vmem((NK, NX, ZR, HD), f32), slices, slices,
            vmem((NY, HD, HD), f32), code, top, code, top, pair, state, rows16, vmem((NH, NK, HD), f32),
            head16, head16, head16, head16, dma((NK, 4)), dma((NK + NH,)),
        ] + [dma(n) for n in counts for _ in range(2)],
        compiler_params=pltpu.CompilerParams(collective_id=0, has_side_effects=True, vmem_limit_bytes=60 << 20),
    )(queries, keys, values, spikes, gain.reshape(NK, HD))
    return attended, cache


def solution(mesh):
    tokens = P(("seq", "head"), None)
    return jax.shard_map(
        per_device, mesh=mesh, in_specs=(tokens, tokens, tokens, tokens, P("head")),
        out_specs=(P("seq", "head"), P("seq", "head", None, None)), check_vma=False,
    )
```

time: 80.7 us -> 65.5 us (0.81)
  Pallas kernels: 76.1 us -> 62.8 us
  local copies, waits for them, and re-layouts: 3.79 us -> 2.02 us
    pallas_call x1, Pallas kernels: 76.1 us -> 62.8 us  [per_device(): pl.pallas_call(kernel, out_shape=(vmem((BLOCK, NK * HD), bf16), vmem((1,...]
    unnamed x4 -> x2, local copies, waits for them, and re-layouts: 3.79 us -> 2.02 us
where the time goes in v2:
time: 65.5 us; the launch traced here: 65.4 us
  Pallas kernels  62.8 us (96%)
  local copies, waits for them, and re-layouts  2.02 us (3%)
    pallas_call x1, Pallas kernels, per_device(): pl.pallas_call(kernel, out_shape=(vmem((BLOCK, NK * HD), bf16), vmem((1,...  62.8 us
    unnamed x2, local copies, waits for them, and re-layouts  2.02 us

profile of v2, /device:TPU:1, one launch (start us, length us, event | category | flops | bytes accessed | tf_op | source)
XLA Modules:
  0.0 65.4 jit_solution(12997778759934177513)
XLA Ops:
  0.6 62.8 %shard_map.68 = (bf16[2048,512]{1,0:T(8,128)(2,1)S(1)}, f32[1,4,128,128]{3,2,1,0:T(8,128)S(1)}) custom-call(bf16[256,4096]{1,0:T(8,128)(2,1)} %q_ref.1, bf16[256,4096]{1,0:T(8,128)(2,1)} %k_ref.1, bf16[256,4096]{1,0:T(8,128)(2,1)} %v_ref.1, s32[256,4096]{1,0:T(8,128)} %sp_ref.1, f32[4,128]{1,0:T(4,128)} %bitcast.1), custom_call_target="tpu_custom_call" | custom-call | tf_op jit(solution)/shard_map/pallas_call | solution.py:295
  63.4 1.3 %copy.9 = bf16[2048,512]{1,0:T(8,128)(2,1)} copy(bf16[2048,512]{1,0:T(8,128)(2,1)S(1)} %get-tuple-element.2) | data formatting | bytes 4194304
  64.7 0.7 %copy.10 = f32[1,4,128,128]{3,2,1,0:T(8,128)} copy(f32[1,4,128,128]{3,2,1,0:T(8,128)S(1)} %get-tuple-element.3) | data formatting | bytes 524288

commit v3 on v2

--- a/solution.py
+++ b/solution.py
@@ -15,11 +15,12 @@
 BLOCK = 2048
 ZR = HD // NZ
 SCALE = HD ** (-0.5)
-LAST = NK - 1
+OWN = 2
 ORDER = (
     "a0", "b0", "s0", "a1", "s1", "c0", "a2", "s2", "c1", "a3", "s3", "c2", "c3", "q3",
-    "l3", "d0", "d1", "l0", "d2", "d3", "x0", "x1", "l1", "y0", "x2", "y1", "l2", "x3",
-    "y2", "f0", "y3", "f1", "f2", "g0", "h0", "g1", "f3", "h1", "g2", "h2", "w3",
+    "l3", "m3", "d0", "d1", "l2", "d2", "d3", "x0", "x1", "l0", "y0", "x2", "y1", "q2",
+    "l1", "x3", "y2", "f0", "y3", "f1", "m2", "g0", "f2", "f3", "h0", "g1", "h1", "w3",
+    "w2",
 )
 f32, bf16 = jnp.float32, jnp.bfloat16
 
@@ -119,7 +120,7 @@
         lax.fori_loop(0, NY, states, 0)
 
     def send_a(k):
-        if k == LAST:
+        if k >= OWN:
             c1[k] = send(S.at[k], RC.at[pl.ds(2 * k, 2)], c1_s.at[k], c1_r.at[k], partner)
         else:
             c1[k] = send(S.at[k, 1 - c], RC.at[2 * k + 1 - c], c1_s.at[k], c1_r.at[k], partner)
@@ -151,22 +152,25 @@
                 scores = dot(qb[k, g], kb[k, g], ((1,), (1,))) * SCALE
                 weights = jnp.where(causal, scores, 0.0).astype(bf16)
                 part = dot(weights, vb[k, g], ((1,), (0,)))
-                if k == LAST:
+                if k >= OWN:
                     part = part + apply_state(qb[k, g], RC[2 * k + cc, yy] * second)
-                    LO[g] = part.astype(bf16)
+                    LO[k - OWN, g] = part.astype(bf16)
                 else:
                     lb[k, g] = part
             return 0
 
-        lax.fori_loop(0, NY, local, 0)
-        if k == LAST:
-            for d in range(1, NH):
-                ql[k].append(send(LO.at[(h + d) % NH], LX.at[h], l_s.at[d - 1], l_r.at[d - 1], at_h(d)))
-            LX[h] = LO[h]
+        lax.fori_loop(0, NY, local, 0, unroll=2)
+
+    def stage_m(k):
+        e = k - OWN
+        for d in range(1, NH):
+            ql[k].append(send(LO.at[e, (h + d) % NH], LX.at[e, h], l_s.at[e, d - 1], l_r.at[e, d - 1], at_h(d)))
+        LX[e, h] = LO[e, h]
 
     def stage_q(k):
-        ql[k] = [send(qb.at[k, (h + d) % NH], QX.at[h], q_s.at[d - 1], q_r.at[d - 1], at_h(d)) for d in range(1, NH)]
-        QX[h] = qb[k, h]
+        e = k - OWN
+        ql[k] = [send(qb.at[k, (h + d) % NH], QX.at[e, h], q_s.at[e, d - 1], q_r.at[e, d - 1], at_h(d)) for d in range(1, NH)]
+        QX[e, h] = qb[k, h]
 
     def stage_d(k):
         arrive(t1[k])
@@ -203,13 +207,13 @@
         arrive(z2[k])
         run = EB[k].reshape(HD, HD)
         for yy in range(NY):
-            if k == LAST:
-                PB[yy] = run
+            if k >= OWN:
+                PB[k - OWN, yy] = run
             else:
                 PC[k, yy], PM[k, yy] = encode(run)
             run = run + T1[k, yy]
         t3[k] = []
-        if k != LAST:
+        if k < OWN:
             for d in range(1, NY):
                 to = (y + d) % NY
                 t3[k].append(send(PC.at[k, to], T3.at[k, y], t3_s.at[k, d - 1, 0], t3_r.at[k, d - 1, 0], at_y(d)))
@@ -241,7 +245,7 @@
                 OB[k, g] = normed(lb[k, g] + apply_state(qb[k, g], PF[k, cc, yy]), GB[g, pl.ds(k, 1), :])
             return 0
 
-        lax.fori_loop(0, NY, final, 0)
+        lax.fori_loop(0, NY, final, 0, unroll=2)
         here = out_ref.at[pl.ds(h * ROWS, ROWS), pl.ds(k * HD, HD)]
         oc[k] = [send(OB.at[k, (h + d) % NH], here, o_s.at[k, d - 1], o_r.at[k, d - 1], at_h(d)) for d in range(1, NH)]
         mine = pltpu.make_async_copy(OB.at[k, h], here, own_sem.at[k])
@@ -250,16 +254,17 @@
 
     def stage_w(k):
         arrive(ql[k])
+        e = k - OWN
 
         def final(yy, _):
             for cc in range(NC):
                 g = yy * NC + cc
-                WO[g] = normed(LX[g].astype(f32) + apply_state(QX[g], PB[yy]), g_ref[pl.ds(k, 1), :])
-            return 0
-
-        lax.fori_loop(0, NY, final, 0)
+                WO[e, g] = normed(LX[e, g].astype(f32) + apply_state(QX[e, g], PB[e, yy]), g_ref[pl.ds(k, 1), :])
+            return 0
+
+        lax.fori_loop(0, NY, final, 0, unroll=2)
         for g in range(NH):
-            mine = pltpu.make_async_copy(WO.at[g], out_ref.at[pl.ds(g * ROWS, ROWS), pl.ds(k * HD, HD)], own_sem.at[NK + g])
+            mine = pltpu.make_async_copy(WO.at[e, g], out_ref.at[pl.ds(g * ROWS, ROWS), pl.ds(k * HD, HD)], own_sem.at[NK + e * NH + g])
             mine.start()
             own.append(mine)
 
@@ -270,7 +275,7 @@
             gains.append(send(g_ref, GB.at[h], g_s.at[d - 1], g_r.at[d - 1], at_h(d)))
 
     stages = {"a": stage_a, "b": stage_b, "s": send_a, "c": stage_c, "l": stage_l, "d": stage_d, "x": stage_x,
-              "y": stage_y, "f": stage_f, "g": stage_g, "h": stage_h, "q": stage_q, "w": stage_w}
+              "y": stage_y, "f": stage_f, "g": stage_g, "h": stage_h, "q": stage_q, "w": stage_w, "m": stage_m}
     for step in ORDER:
         stages[step[0]](int(step[1]))
     for cp in own:
@@ -289,9 +294,9 @@
     code = vmem((NK, NY, HD, HD), jnp.int16)
     top = vmem((NK, NY, 1, HD), f32)
     slices = vmem((NK, NZ, ZR, HD), f32)
-    rows16, head16 = vmem((NK, NH, ROWS, HD), bf16), vmem((NH, ROWS, HD), bf16)
-    over_y, over_z, over_h = (NK, NY - 1, 2), (NK, NZ - 1), (NH - 1,)
-    counts = over_h, (NK,), over_y, over_z, (NK, NX - 1), over_z, over_y, (NK,), (NK, NH - 1), over_h, over_h
+    rows16, head16 = vmem((NK, NH, ROWS, HD), bf16), vmem((NK - OWN, NH, ROWS, HD), bf16)
+    over_y, over_z, over_h = (NK, NY - 1, 2), (NK, NZ - 1), (NK - OWN, NH - 1)
+    counts = (NH - 1,), (NK,), over_y, over_z, (NK, NX - 1), over_z, over_y, (NK,), (NK, NH - 1), over_h, over_h
     attended, cache = pl.pallas_call(
         kernel,
         out_shape=(vmem((BLOCK, NK * HD), bf16), vmem((1, NK, HD, HD), f32)),
@@ -301,8 +306,8 @@
             rows16, rows16, rows16, vmem((NK, NH, ROWS, HD), jnp.int32), vmem((NK, NH, ROWS, HD), f32),
             pair, vmem((NK * NC, NY, HD, HD), f32), code, top, code, top, state,
             slices, slices, vmem((NK, ZR, HD), f32), vmem((NK, NX, ZR, HD), f32), slices, slices,
-            vmem((NY, HD, HD), f32), code, top, code, top, pair, state, rows16, vmem((NH, NK, HD), f32),
-            head16, head16, head16, head16, dma((NK, 4)), dma((NK + NH,)),
+            vmem((NK - OWN, NY, HD, HD), f32), code, top, code, top, pair, state, rows16, vmem((NH, NK, HD), f32),
+            head16, head16, head16, head16, dma((NK, 4)), dma((NK + (NK - OWN) * NH,)),
         ] + [dma(n) for n in counts for _ in range(2)],
         compiler_params=pltpu.CompilerParams(collective_id=0, has_side_effects=True, vmem_limit_bytes=60 << 20),
     )(queries, keys, values, spikes, gain.reshape(NK, HD))

time: 65.5 us -> 64.9 us (level)
  Pallas kernels: 62.8 us -> 62.1 us
    pallas_call x1, Pallas kernels: 62.8 us -> 62.1 us  [per_device(): pl.pallas_call(kernel, out_shape=(vmem((BLOCK, NK * HD), bf16), vmem((1,...]
where the time goes in v3:
time: 64.9 us; the launch traced here: 64.7 us
  Pallas kernels  62.1 us (96%)
  local copies, waits for them, and re-layouts  2.02 us (3%)
    pallas_call x1, Pallas kernels, per_device(): pl.pallas_call(kernel, out_shape=(vmem((BLOCK, NK * HD), bf16), vmem((1,...  62.1 us
    unnamed x2, local copies, waits for them, and re-layouts  2.02 us

profile of v3, /device:TPU:1, one launch (start us, length us, event | category | flops | bytes accessed | tf_op | source)
XLA Modules:
  0.0 64.7 jit_solution(2027452348065181010)
XLA Ops:
  0.6 62.1 %shard_map.68 = (bf16[2048,512]{1,0:T(8,128)(2,1)S(1)}, f32[1,4,128,128]{3,2,1,0:T(8,128)S(1)}) custom-call(bf16[256,4096]{1,0:T(8,128)(2,1)} %q_ref.1, bf16[256,4096]{1,0:T(8,128)(2,1)} %k_ref.1, bf16[256,4096]{1,0:T(8,128)(2,1)} %v_ref.1, s32[256,4096]{1,0:T(8,128)} %sp_ref.1, f32[4,128]{1,0:T(4,128)} %bitcast.1), custom_call_target="tpu_custom_call" | custom-call | tf_op jit(solution)/shard_map/pallas_call | solution.py:300
  62.7 1.3 %copy.9 = bf16[2048,512]{1,0:T(8,128)(2,1)} copy(bf16[2048,512]{1,0:T(8,128)(2,1)S(1)} %get-tuple-element.2) | data formatting | bytes 4194304
  64.0 0.7 %copy.10 = f32[1,4,128,128]{3,2,1,0:T(8,128)} copy(f32[1,4,128,128]{3,2,1,0:T(8,128)S(1)} %get-tuple-element.3) | data formatting | bytes 524288
